TPU v7x, 256 devices: a whole 4x4x8 slice. The times are simulated.
256 devices in a mesh: dom: 64 (over z, y, core), chan: 4 (over x).
Axes of the slice: x: 4, y: 4, z: 8, core: 2. Of those that a mesh axis runs over, the one named last changes fastest.
Arguments:
- features: bfloat16 [256, 65536], P('chan', 'dom'), may hold values from -6 to 6
- cotangent: bfloat16 [256, 65536], P('chan', 'dom'), may hold values from -6 to 6
- weights: bfloat16 [9, 256, 256], P(None, 'chan'), may hold values from -0.375 to 0.375
- tile_values: float32 [4096, 128, 128], P('dom'), may hold values from -0.046875 to 0.046875
- tile_cols: int32 [64, 8, 8], P('dom'), may hold values from 0 to 11, as said below
- send_list: int32 [64, 4, 128], P('dom'), may hold values from 0 to 1023
Outputs:
- input_grad: float32 [256, 65536], P('chan', 'dom')
- weight_grad: float32 [9, 256, 256], P(None, None, 'chan')
Inputs may be any that keep to these rules, and one draw needn't show every extreme that they name: `tile_cols`: values below 8 are blocks of the partition's own nodes; 8 + s is the block received from neighbour slot s. Tile 0 of row block r has column block r.
All inputs are finite; a program needn't handle non-finite values.
Results may differ from a plain program's by a relative error of at most 0.0003.
Values may be sent and summed in bfloat16 or wider, within the bound.
A program may use at most 128 MiB of HBM per device.

v0:
```python
import jax
import jax.numpy as jnp
from jax import lax
from jax.sharding import PartitionSpec as P

NEIGHBOUR_SHIFTS = (1, -1, 2, -2)


def from_behind(block, axis, distance):
    devices = range(lax.axis_size(axis))
    route = [((i - distance) % len(devices), i) for i in devices]
    return lax.ppermute(block, axis, route)


def exchange_rows(outgoing):
    received = [
        from_behind(outgoing[:, slot_index], "dom", offset)
        for slot_index, offset in enumerate(NEIGHBOUR_SHIFTS)
    ]
    return received


def apply_operator(field_in, tile_values, tile_cols, send_list):
    channels, local_nodes = field_in.shape
    tile_size = tile_values.shape[-1]
    per_row = tile_cols.shape[-1]
    outgoing = jnp.take(field_in, send_list[0], axis=1)
    received = exchange_rows(outgoing)
    extended = jnp.concatenate([field_in] + received, axis=1)
    blocks = extended.reshape(channels, -1, tile_size)
    picked = jnp.take(blocks, tile_cols.reshape(-1), axis=1)
    product = jnp.einsum("ctj,tjk->ctk", picked, tile_values, precision=lax.Precision.HIGHEST)
    return (
        product.reshape(channels, -1, per_row, tile_size).sum(axis=2).reshape(channels, local_nodes)
    )


def local(features, cotangent, weights, tile_values, tile_cols, send_list):
    top_order = weights.shape[0] - 1
    local_nodes = features.shape[1]

    def operator_on(field_in):
        return apply_operator(field_in, tile_values, tile_cols, send_list)

    feat_all, cot_all = (
        lax.all_gather(features, "chan", axis=0, tiled=True),
        lax.all_gather(cotangent, "chan", axis=0, tiled=True),
    )
    feat_wide = feat_all.astype(jnp.float32)

    def mixed_term(order_index):
        return jnp.dot(weights[order_index], cot_all, preferred_element_type=jnp.float32)

    def grad_term(state):
        return lax.dot_general(
            feat_wide, state, (((1,), (1,)), ((), ())), precision=lax.Precision.HIGHEST
        )

    cheb_prev = cotangent.astype(jnp.float32)
    grad_terms = [grad_term(cheb_prev)]
    cheb_now = operator_on(cheb_prev)
    grad_terms.append(grad_term(cheb_now))
    for order_index in range(2, top_order + 1):
        cheb_prev, cheb_now = (cheb_now, 2.0 * operator_on(cheb_now) - cheb_prev)
        grad_terms.append(grad_term(cheb_now))
    current = mixed_term(top_order)
    clen_later = jnp.zeros_like(current)
    for order_index in range(top_order - 1, 0, -1):
        current, clen_later = (
            mixed_term(order_index) + 2.0 * operator_on(current) - clen_later,
            current,
        )
    input_grad = mixed_term(0) + operator_on(current) - clen_later
    local_grads = jnp.stack(grad_terms)
    summed = lax.psum(local_grads, "dom")
    nodes_all = lax.axis_size("dom") * local_nodes
    return (input_grad, summed * float(nodes_all) ** (-0.5))


def solution(mesh):
    placed = (
        P("chan", "dom"),
        P("chan", "dom"),
        P(None, "chan", None),
        P("dom", None, None),
        P("dom", None, None),
        P("dom", None, None),
    )
    return jax.shard_map(
        local,
        mesh=mesh,
        in_specs=placed,
        out_specs=(P("chan", "dom"), P(None, None, "chan")),
        check_vma=False,
    )
```

profile of v0, /device:TPU:2, one launch (start us, length us, event | category | flops | bytes accessed | tf_op | source)
XLA Modules:
  0.0 664.3 jit_solution(9862079954037837758)
XLA Ops:
  8.6 13.7 %all_gather.6 = bf16[256,1024]{1,0:T(8,128)(2,1)S(1)} all-gather(bf16[64,1024]{1,0:T(8,128)(2,1)} %param.11), channel_id=1, replica_groups=mesh['dom'=64,'chan'=4] {'chan'}, dimensions={0}, use_global_device_ids=true | all-gather | bytes 655360 | tf_op jit(solution)/shard_map/all_gather | solution.py:47
  38.1 12.8 %all_gather.7 = bf16[256,1024]{1,0:T(8,128)(2,1)S(1)} all-gather(bf16[64,1024]{1,0:T(8,128)(2,1)S(1)} %copy-done.13), channel_id=1, replica_groups=mesh['dom'=64,'chan'=4] {'chan'}, dimensions={0}, use_global_device_ids=true | all-gather | bytes 655360 | tf_op jit(solution)/shard_map/all_gather | solution.py:46
  57.3 7.7 %collective-permute-done.34 = f32[64,128]{0,1:T(8,128)S(1)} collective-permute-done((f32[64,128]{0,1:T(8,128)S(1)}, f32[64,128]{0,1:T(8,128)S(1)}, u32[]{:S(2)}, u32[]{:S(2)}) %collective-permute-start.34) | collective-permute-done | bytes 32800 | tf_op jit(solution)/shard_map/ppermute | solution.py:12
  70.4 6.4 bitcast_reduce_fusion.7
  88.4 6.7 %bitcast_reduce_fusion.15 = f32[64,8,128]{2,0,1:T(8,128)S(1)} fusion(f32[64,128,128]{2,1,0:T(8,128)} %param.13, f32[64,64,128]{2,1,0:T(8,128)} %gather_fusion.1, pred[64]{0:T(512)(128)(4,1)S(1)} %compare_and_fusion), kind=kOutput, calls=%fused_computation.47 | convolution fusion | flops 806289408 | bytes 6553664 | tf_op jit(solution)/shard_map/ctj,tjk->ctk/dot_general | solution.py:32
  123.1 6.7 %bitcast_reduce_fusion.14 = f32[64,8,128]{2,0,1:T(8,128)S(1)} fusion(f32[64,128,128]{2,1,0:T(8,128)} %param.13, f32[64,64,128]{2,1,0:T(8,128)} %gather_fusion.3, pred[64]{0:T(512)(128)(4,1)S(1)} %compare_and_fusion), kind=kOutput, calls=%fused_computation.46 | convolution fusion | flops 806289408 | bytes 6553664 | tf_op jit(solution)/shard_map/ctj,tjk->ctk/dot_general | solution.py:32
  152.7 6.7 %bitcast_reduce_fusion.6 = f32[64,8,128]{2,0,1:T(8,128)S(1)} fusion(f32[64,128,128]{2,1,0:T(8,128)} %param.13, f32[64,64,128]{2,1,0:T(8,128)} %gather_fusion.19, pred[64]{0:T(512)(128)(4,1)S(1)} %compare_and_fusion), kind=kOutput, calls=%fused_computation.38 | convolution fusion | flops 806289408 | bytes 6553664 | tf_op jit(solution)/shard_map/ctj,tjk->ctk/dot_general | solution.py:32
  179.7 6.7 %bitcast_reduce_fusion.13 = f32[64,8,128]{2,0,1:T(8,128)S(1)} fusion(f32[64,128,128]{2,1,0:T(8,128)} %param.13, f32[64,64,128]{2,1,0:T(8,128)} %gather_fusion.5, pred[64]{0:T(512)(128)(4,1)S(1)} %compare_and_fusion), kind=kOutput, calls=%fused_computation.45 | convolution fusion | flops 806289408 | bytes 6553664 | tf_op jit(solution)/shard_map/ctj,tjk->ctk/dot_general | solution.py:32
  198.1 5.6 collective-permute-start.15
  210.0 6.7 %bitcast_reduce_fusion.5 = f32[64,8,128]{2,0,1:T(8,128)S(1)} fusion(f32[64,128,128]{2,1,0:T(8,128)} %param.13, f32[64,64,128]{2,1,0:T(8,128)} %gather_fusion.21, pred[64]{0:T(512)(128)(4,1)S(1)} %compare_and_fusion), kind=kOutput, calls=%fused_computation.37 | convolution fusion | flops 806289408 | bytes 6553664 | tf_op jit(solution)/shard_map/ctj,tjk->ctk/dot_general | solution.py:32
  230.5 5.8 collective-permute-start.47
  242.1 6.7 %bitcast_reduce_fusion.12 = f32[64,8,128]{2,0,1:T(8,128)S(1)} fusion(f32[64,128,128]{2,1,0:T(8,128)} %param.13, f32[64,64,128]{2,1,0:T(8,128)} %gather_fusion.7, pred[64]{0:T(512)(128)(4,1)S(1)} %compare_and_fusion), kind=kOutput, calls=%fused_computation.44 | convolution fusion | flops 806289408 | bytes 6553664 | tf_op jit(solution)/shard_map/ctj,tjk->ctk/dot_general | solution.py:32
  270.7 6.7 %bitcast_reduce_fusion.4 = f32[64,8,128]{2,0,1:T(8,128)S(1)} fusion(f32[64,128,128]{2,1,0:T(8,128)} %param.13, f32[64,64,128]{2,1,0:T(8,128)} %gather_fusion.23, pred[64]{0:T(512)(128)(4,1)S(1)} %compare_and_fusion), kind=kOutput, calls=%fused_computation.36 | convolution fusion | flops 806289408 | bytes 6553664 | tf_op jit(solution)/shard_map/ctj,tjk->ctk/dot_general | solution.py:32
  297.4 6.7 %bitcast_reduce_fusion.11 = f32[64,8,128]{2,0,1:T(8,128)S(1)} fusion(f32[64,128,128]{2,1,0:T(8,128)} %param.13, f32[64,64,128]{2,1,0:T(8,128)} %gather_fusion.9, pred[64]{0:T(512)(128)(4,1)S(1)} %compare_and_fusion), kind=kOutput, calls=%fused_computation.43 | convolution fusion | flops 806289408 | bytes 6553664 | tf_op jit(solution)/shard_map/ctj,tjk->ctk/dot_general | solution.py:32
  325.5 6.7 %bitcast_reduce_fusion.3 = f32[64,8,128]{2,0,1:T(8,128)S(1)} fusion(f32[64,128,128]{2,1,0:T(8,128)} %param.13, f32[64,64,128]{2,1,0:T(8,128)} %gather_fusion.25, pred[64]{0:T(512)(128)(4,1)S(1)} %compare_and_fusion), kind=kOutput, calls=%fused_computation.35 | convolution fusion | flops 806289408 | bytes 6553664 | tf_op jit(solution)/shard_map/ctj,tjk->ctk/dot_general | solution.py:32
  341.6 5.8 collective-permute-start.55
  349.5 6.7 %bitcast_reduce_fusion.10 = f32[64,8,128]{2,0,1:T(8,128)S(1)} fusion(f32[64,128,128]{2,1,0:T(8,128)} %param.13, f32[64,64,128]{2,1,0:T(8,128)} %gather_fusion.11, pred[64]{0:T(512)(128)(4,1)S(1)} %compare_and_fusion), kind=kOutput, calls=%fused_computation.42 | convolution fusion | flops 806289408 | bytes 6553664 | tf_op jit(solution)/shard_map/ctj,tjk->ctk/dot_general | solution.py:32
  378.1 6.7 %bitcast_reduce_fusion.2 = f32[64,8,128]{2,0,1:T(8,128)S(1)} fusion(f32[64,128,128]{2,1,0:T(8,128)} %param.13, f32[64,64,128]{2,1,0:T(8,128)} %gather_fusion.27, pred[64]{0:T(512)(128)(4,1)S(1)} %compare_and_fusion), kind=kOutput, calls=%fused_computation.34 | convolution fusion | flops 806289408 | bytes 6553664 | tf_op jit(solution)/shard_map/ctj,tjk->ctk/dot_general | solution.py:32
  404.7 6.7 %bitcast_reduce_fusion.9 = f32[64,8,128]{2,0,1:T(8,128)S(1)} fusion(f32[64,128,128]{2,1,0:T(8,128)} %param.13, f32[64,64,128]{2,1,0:T(8,128)} %gather_fusion.13, pred[64]{0:T(512)(128)(4,1)S(1)} %compare_and_fusion), kind=kOutput, calls=%fused_computation.41 | convolution fusion | flops 806289408 | bytes 6553664 | tf_op jit(solution)/shard_map/ctj,tjk->ctk/dot_general | solution.py:32
  433.5 6.7 %bitcast_reduce_fusion.1 = f32[64,8,128]{2,0,1:T(8,128)S(1)} fusion(f32[64,128,128]{2,1,0:T(8,128)} %param.13, f32[64,64,128]{2,1,0:T(8,128)} %gather_fusion.29, pred[64]{0:T(512)(128)(4,1)S(1)} %compare_and_fusion), kind=kOutput, calls=%fused_computation.33 | convolution fusion | flops 806289408 | bytes 6553664 | tf_op jit(solution)/shard_map/ctj,tjk->ctk/dot_general | solution.py:32
  450.4 5.6 collective-permute-start.63
  465.5 6.7 %bitcast_reduce_fusion = f32[64,8,128]{2,0,1:T(8,128)S(1)} fusion(f32[64,128,128]{2,1,0:T(8,128)} %param.13, f32[64,64,128]{2,1,0:T(8,128)} %gather_fusion.31, pred[64]{0:T(512)(128)(4,1)S(1)} %compare_and_fusion), kind=kOutput, calls=%fused_computation.32 | convolution fusion | flops 806289408 | bytes 6553664 | tf_op jit(solution)/shard_map/ctj,tjk->ctk/dot_general | solution.py:32
  473.8 6.7 %bitcast_reduce_fusion.8 = f32[64,8,128]{2,0,1:T(8,128)S(1)} fusion(f32[64,128,128]{2,1,0:T(8,128)} %param.13, f32[64,64,128]{2,1,0:T(8,128)} %gather_fusion.15, pred[64]{0:T(512)(128)(4,1)S(1)} %compare_and_fusion), kind=kOutput, calls=%fused_computation.40 | convolution fusion | flops 806289408 | bytes 6553664 | tf_op jit(solution)/shard_map/ctj,tjk->ctk/dot_general | solution.py:32
  482.2 172.9 %all-reduce.2.cloned.1.call-done = f32[9,256,64]{1,2,0:T(8,128)} async-done(((f32[9,256,64]{1,2,0:T(8,128)}), f32[9,256,64]{1,2,0:T(8,128)}) %all-reduce.2.cloned.1.call-update) | async-done | bytes 589840 | tf_op jit(solution)/shard_map/psum | solution.py:75
  (368 shorter events, 312.0 us)
Async XLA Ops:
  7.2 647.9 %all-reduce.2.cloned.1.call-start = ((), (), s32[]{:S(2)}) async-start(), calls=%async_computation | async-start | bytes 1179648 | tf_op jit(solution)/shard_map/psum | solution.py:75
  26.1 52.7 %collective-permute-start = (f32[64,128]{1,0:T(8,128)}, f32[64,128]{1,0:T(8,128)}, u32[]{:S(2)}, u32[]{:S(2)}) collective-permute-start(f32[64,128]{1,0:T(8,128)} %get-tuple-element.67), channel_id=1, source_target_pairs={{252,0},{0,4},{4,8},{8,12},{12,16},{16,20},{20,24},{24,28},{28,32}... | collective-permute-start | bytes 98312 | tf_op jit(solution)/shard_map/ppermute | solution.py:12
  26.1 54.0 %collective-permute-start.1 = (f32[64,128]{1,0:T(8,128)}, f32[64,128]{1,0:T(8,128)}, u32[]{:S(2)}, u32[]{:S(2)}) collective-permute-start(f32[64,128]{1,0:T(8,128)} %get-tuple-element.66), channel_id=1, source_target_pairs={{4,0},{8,4},{12,8},{16,12},{20,16},{24,20},{28,24},{32,28},{36,32}... | collective-permute-start | bytes 98312 | tf_op jit(solution)/shard_map/ppermute | solution.py:12
  31.2 50.4 %collective-permute-start.2 = (f32[64,128]{1,0:T(8,128)}, f32[64,128]{1,0:T(8,128)}, u32[]{:S(2)}, u32[]{:S(2)}) collective-permute-start(f32[64,128]{1,0:T(8,128)} %get-tuple-element.65), channel_id=1, source_target_pairs={{248,0},{252,4},{0,8},{4,12},{8,16},{12,20},{16,24},{20,28},{24,32... | collective-permute-start | bytes 98312 | tf_op jit(solution)/shard_map/ppermute | solution.py:12
  31.2 52.8 %collective-permute-start.3 = (f32[64,128]{1,0:T(8,128)}, f32[64,128]{1,0:T(8,128)}, u32[]{:S(2)}, u32[]{:S(2)}) collective-permute-start(f32[64,128]{1,0:T(8,128)} %get-tuple-element.64), channel_id=1, source_target_pairs={{8,0},{12,4},{16,8},{20,12},{24,16},{28,20},{32,24},{36,28},{40,32... | collective-permute-start | bytes 98312 | tf_op jit(solution)/shard_map/ppermute | solution.py:12
  132.8 34.2 %collective-permute-start.8 = (f32[64,128]{1,0:T(8,128)}, f32[64,128]{1,0:T(8,128)S(1)}, u32[]{:S(2)}, u32[]{:S(2)}) collective-permute-start(f32[64,128]{1,0:T(8,128)} %get-tuple-element.59), channel_id=1, source_target_pairs={{252,0},{0,4},{4,8},{8,12},{12,16},{16,20},{20,24},{24,28},{28,32}... | collective-permute-start | bytes 98312 | tf_op jit(solution)/shard_map/ppermute | solution.py:12
  132.8 39.2 %collective-permute-start.9 = (f32[64,128]{1,0:T(8,128)}, f32[64,128]{1,0:T(8,128)S(1)}, u32[]{:S(2)}, u32[]{:S(2)}) collective-permute-start(f32[64,128]{1,0:T(8,128)} %get-tuple-element.58), channel_id=1, source_target_pairs={{4,0},{8,4},{12,8},{16,12},{20,16},{24,20},{28,24},{32,28},{36,32}... | collective-permute-start | bytes 98312 | tf_op jit(solution)/shard_map/ppermute | solution.py:12
  139.3 32.7 %collective-permute-start.10 = (f32[64,128]{1,0:T(8,128)}, f32[64,128]{1,0:T(8,128)S(1)}, u32[]{:S(2)}, u32[]{:S(2)}) collective-permute-start(f32[64,128]{1,0:T(8,128)} %get-tuple-element.57), channel_id=1, source_target_pairs={{248,0},{252,4},{0,8},{4,12},{8,16},{12,20},{16,24},{20,28},{24,32... | collective-permute-start | bytes 98312 | tf_op jit(solution)/shard_map/ppermute | solution.py:12
  140.8 36.8 %collective-permute-start.11 = (f32[64,128]{1,0:T(8,128)}, f32[64,128]{1,0:T(8,128)S(1)}, u32[]{:S(2)}, u32[]{:S(2)}) collective-permute-start(f32[64,128]{1,0:T(8,128)} %get-tuple-element.56), channel_id=1, source_target_pairs={{8,0},{12,4},{16,8},{20,12},{24,16},{28,20},{32,24},{36,28},{40,32... | collective-permute-start | bytes 98312 | tf_op jit(solution)/shard_map/ppermute | solution.py:12
  172.1 33.0 %collective-permute-start.43 = (f32[64,128]{0,1:T(8,128)}, f32[64,128]{0,1:T(8,128)}, u32[]{:S(2)}, u32[]{:S(2)}) collective-permute-start(f32[64,128]{0,1:T(8,128)} %get-tuple-element.24), channel_id=1, source_target_pairs={{8,0},{12,4},{16,8},{20,12},{24,16},{28,20},{32,24},{36,28},{40,32... | collective-permute-start | bytes 98312 | tf_op jit(solution)/shard_map/ppermute | solution.py:12
  190.1 38.4 %collective-permute-start.13 = (f32[64,128]{1,0:T(8,128)}, f32[64,128]{1,0:T(8,128)S(1)}, u32[]{:S(2)}, u32[]{:S(2)}) collective-permute-start(f32[64,128]{1,0:T(8,128)} %get-tuple-element.54), channel_id=1, source_target_pairs={{4,0},{8,4},{12,8},{16,12},{20,16},{24,20},{28,24},{32,28},{36,32}... | collective-permute-start | bytes 98312 | tf_op jit(solution)/shard_map/ppermute | solution.py:12
  196.6 33.9 %collective-permute-start.14 = (f32[64,128]{1,0:T(8,128)}, f32[64,128]{1,0:T(8,128)}, u32[]{:S(2)}, u32[]{:S(2)}) collective-permute-start(f32[64,128]{1,0:T(8,128)} %get-tuple-element.53), channel_id=1, source_target_pairs={{248,0},{252,4},{0,8},{4,12},{8,16},{12,20},{16,24},{20,28},{24,32... | collective-permute-start | bytes 98312 | tf_op jit(solution)/shard_map/ppermute | solution.py:12
  198.1 39.6 %collective-permute-start.15 = (f32[64,128]{1,0:T(8,128)}, f32[64,128]{1,0:T(8,128)}, u32[]{:S(2)}, u32[]{:S(2)}) collective-permute-start(f32[64,128]{1,0:T(8,128)} %get-tuple-element.52), channel_id=1, source_target_pairs={{8,0},{12,4},{16,8},{20,12},{24,16},{28,20},{32,24},{36,28},{40,32... | collective-permute-start | bytes 98312 | tf_op jit(solution)/shard_map/ppermute | solution.py:12
  222.8 36.3 %collective-permute-start.45 = (f32[64,128]{0,1:T(8,128)}, f32[64,128]{0,1:T(8,128)S(1)}, u32[]{:S(2)}, u32[]{:S(2)}) collective-permute-start(f32[64,128]{0,1:T(8,128)} %get-tuple-element.22), channel_id=1, source_target_pairs={{4,0},{8,4},{12,8},{16,12},{20,16},{24,20},{28,24},{32,28},{36,32}... | collective-permute-start | bytes 98312 | tf_op jit(solution)/shard_map/ppermute | solution.py:12
  230.5 35.3 %collective-permute-start.47 = (f32[64,128]{0,1:T(8,128)}, f32[64,128]{0,1:T(8,128)}, u32[]{:S(2)}, u32[]{:S(2)}) collective-permute-start(f32[64,128]{0,1:T(8,128)} %get-tuple-element.20), channel_id=1, source_target_pairs={{8,0},{12,4},{16,8},{20,12},{24,16},{28,20},{32,24},{36,28},{40,32... | collective-permute-start | bytes 98312 | tf_op jit(solution)/shard_map/ppermute | solution.py:12
  252.6 34.9 %collective-permute-start.17 = (f32[64,128]{1,0:T(8,128)}, f32[64,128]{1,0:T(8,128)}, u32[]{:S(2)}, u32[]{:S(2)}) collective-permute-start(f32[64,128]{1,0:T(8,128)} %get-tuple-element.50), channel_id=1, source_target_pairs={{4,0},{8,4},{12,8},{16,12},{20,16},{24,20},{28,24},{32,28},{36,32}... | collective-permute-start | bytes 98312 | tf_op jit(solution)/shard_map/ppermute | solution.py:12
  259.7 34.8 %collective-permute-start.19 = (f32[64,128]{1,0:T(8,128)}, f32[64,128]{1,0:T(8,128)}, u32[]{:S(2)}, u32[]{:S(2)}) collective-permute-start(f32[64,128]{1,0:T(8,128)} %get-tuple-element.48), channel_id=1, source_target_pairs={{8,0},{12,4},{16,8},{20,12},{24,16},{28,20},{32,24},{36,28},{40,32... | collective-permute-start | bytes 98312 | tf_op jit(solution)/shard_map/ppermute | solution.py:12
  307.3 34.2 %collective-permute-start.21 = (f32[64,128]{1,0:T(8,128)S(1)}, f32[64,128]{1,0:T(8,128)S(1)}, u32[]{:S(2)}, u32[]{:S(2)}) collective-permute-start(f32[64,128]{1,0:T(8,128)S(1)} %get-tuple-element.46), channel_id=1, source_target_pairs={{4,0},{8,4},{12,8},{16,12},{20,16},{24,20},{28,24},{32,28},{36,32}... | collective-permute-start | bytes 98312 | tf_op jit(solution)/shard_map/ppermute | solution.py:12
  314.4 33.0 %collective-permute-start.23 = (f32[64,128]{1,0:T(8,128)S(1)}, f32[64,128]{1,0:T(8,128)S(1)}, u32[]{:S(2)}, u32[]{:S(2)}) collective-permute-start(f32[64,128]{1,0:T(8,128)S(1)} %get-tuple-element.44), channel_id=1, source_target_pairs={{8,0},{12,4},{16,8},{20,12},{24,16},{28,20},{32,24},{36,28},{40,32... | collective-permute-start | bytes 98312 | tf_op jit(solution)/shard_map/ppermute | solution.py:12
  359.9 34.9 %collective-permute-start.25 = (f32[64,128]{1,0:T(8,128)}, f32[64,128]{1,0:T(8,128)}, u32[]{:S(2)}, u32[]{:S(2)}) collective-permute-start(f32[64,128]{1,0:T(8,128)} %get-tuple-element.42), channel_id=1, source_target_pairs={{4,0},{8,4},{12,8},{16,12},{20,16},{24,20},{28,24},{32,28},{36,32}... | collective-permute-start | bytes 98312 | tf_op jit(solution)/shard_map/ppermute | solution.py:12
  367.1 34.8 %collective-permute-start.27 = (f32[64,128]{1,0:T(8,128)}, f32[64,128]{1,0:T(8,128)}, u32[]{:S(2)}, u32[]{:S(2)}) collective-permute-start(f32[64,128]{1,0:T(8,128)} %get-tuple-element.40), channel_id=1, source_target_pairs={{8,0},{12,4},{16,8},{20,12},{24,16},{28,20},{32,24},{36,28},{40,32... | collective-permute-start | bytes 98312 | tf_op jit(solution)/shard_map/ppermute | solution.py:12
  395.6 33.0 %collective-permute-start.59 = (f32[64,128]{0,1:T(8,128)}, f32[64,128]{0,1:T(8,128)}, u32[]{:S(2)}, u32[]{:S(2)}) collective-permute-start(f32[64,128]{0,1:T(8,128)} %get-tuple-element.8), channel_id=1, source_target_pairs={{8,0},{12,4},{16,8},{20,12},{24,16},{28,20},{32,24},{36,28},{40,32... | collective-permute-start | bytes 98312 | tf_op jit(solution)/shard_map/ppermute | solution.py:12
  415.2 34.4 %collective-permute-start.29 = (f32[64,128]{1,0:T(8,128)}, f32[64,128]{1,0:T(8,128)}, u32[]{:S(2)}, u32[]{:S(2)}) collective-permute-start(f32[64,128]{1,0:T(8,128)} %get-tuple-element.38), channel_id=1, source_target_pairs={{4,0},{8,4},{12,8},{16,12},{20,16},{24,20},{28,24},{32,28},{36,32}... | collective-permute-start | bytes 98312 | tf_op jit(solution)/shard_map/ppermute | solution.py:12
  422.4 34.4 %collective-permute-start.31 = (f32[64,128]{1,0:T(8,128)}, f32[64,128]{1,0:T(8,128)}, u32[]{:S(2)}, u32[]{:S(2)}) collective-permute-start(f32[64,128]{1,0:T(8,128)} %get-tuple-element.36), channel_id=1, source_target_pairs={{8,0},{12,4},{16,8},{20,12},{24,16},{28,20},{32,24},{36,28},{40,32... | collective-permute-start | bytes 98312 | tf_op jit(solution)/shard_map/ppermute | solution.py:12
  (57 other events, 1124.3 us)
Sparse Core Ops, SparseCore 0:
  473.9 181.1 all-reduce.1
where the time goes:
time: 673 us; the launch traced here: 664 us
  waiting for transfers between devices  187 us (28%)
  starting transfers between devices  164 us (24%)
  matrix products  131 us (19%)
  local copies, waits for them, and re-layouts  127 us (19%)
  blocking collectives  26.5 us (4%)
  between operations  15.7 us (2%)
  other arithmetic  13 us (2%)
    psum x1, waiting for transfers between devices, local(): summed = lax.psum(local_grads, 'dom')  173 us
    ppermute x64, starting transfers between devices, from_behind(): return lax.ppermute(block, axis, route)  163 us
    dot_general x16, matrix products, apply_operator(): jnp.einsum('ctj,tjk->ctk', picked, tile_values, precision=lax.Precision.H...  107 us
    unnamed x82, local copies, waits for them, and re-layouts  37.6 us
    gather x16, local copies, waits for them, and re-layouts, apply_operator(): picked = jnp.take(blocks, tile_cols.reshape(-1), axis=1)  31.3 us
    gather x24, local copies, waits for them, and re-layouts, apply_operator(): outgoing = jnp.take(field_in, send_list[0], axis=1)  18 us
    concatenate x16, local copies, waits for them, and re-layouts, apply_operator(): extended = jnp.concatenate([field_in] + received, axis=1)  14.5 us
    ppermute x64, waiting for transfers between devices, from_behind(): return lax.ppermute(block, axis, route)  14 us
  transfers between devices with their start and end apart: 65, of which 4 were waited for; matrix products, arithmetic and copies ran while one was open for 36% of the time, Pallas kernels for 0%

commit v1 on v0

--- a/solution.py
+++ b/solution.py
@@ -36,6 +36,18 @@
 
 
 def local(features, cotangent, weights, tile_values, tile_cols, send_list):
+
+    def steps_all_take(array_in):
+        n_peers_all = lax.axis_size("chan")
+        history = []
+        s = 0
+        while s < array_in.ndim:
+            history.append(n_peers_all if s == 0 else 1)
+            s += 1
+        return lax.all_to_all(
+            jnp.tile(array_in, history), "chan", concat_axis=0, tiled=True, split_axis=0
+        )
+
     top_order = weights.shape[0] - 1
     local_nodes = features.shape[1]
 
@@ -44,7 +56,7 @@
 
     feat_all, cot_all = (
         lax.all_gather(features, "chan", axis=0, tiled=True),
-        lax.all_gather(cotangent, "chan", axis=0, tiled=True),
+        steps_all_take(cotangent),
     )
     feat_wide = feat_all.astype(jnp.float32)
 

time: 673 us -> 611 us (0.908)
  local copies, waits for them, and re-layouts: 127 us -> 74.4 us
  blocking collectives: 26.5 us -> 13.4 us
  starting transfers between devices: 164 us -> 176 us
    unnamed x82 -> x80, local copies, waits for them, and re-layouts: 37.6 us -> 9.93 us
    all_gather x1 -> x0, blocking collectives: 13.7 us -> none  [local(): lax.all_gather(cotangent, 'chan', axis=0, tiled=True)]
    concatenate x16, local copies, waits for them, and re-layouts: 14.5 us -> 1.94 us  [apply_operator(): extended = jnp.concatenate([field_in] + received, axis=1)]
    psum x1, waiting for transfers between devices: 173 us -> 163 us  [local(): summed = lax.psum(local_grads, 'dom')]
    ppermute x64, waiting for transfers between devices: 14 us -> 22.3 us  [from_behind(): return lax.ppermute(block, axis, route)]
    squeeze x16, local copies, waits for them, and re-layouts: 8.17 us -> 0.91 us  [exchange_rows(): outgoing[:, slot_index]]
  transfers between devices with their start and end apart: 65 -> 66, of which waited for: 4 -> 18; matrix products, arithmetic and copies ran while one was open for 36% -> 26% of each run, Pallas kernels for 0% -> 0%
where the time goes in v1:
time: 611 us; the launch traced here: 602 us
  waiting for transfers between devices  185 us (30%)
  starting transfers between devices  176 us (29%)
  matrix products  126 us (21%)
  local copies, waits for them, and re-layouts  74.4 us (12%)
  between operations  15.8 us (3%)
  blocking collectives  13.4 us (2%)
  other arithmetic  11.6 us (2%)
    ppermute x64, starting transfers between devices, from_behind(): return lax.ppermute(block, axis, route)  170 us
    psum x1, waiting for transfers between devices, local(): summed = lax.psum(local_grads, 'dom')  163 us
    dot_general x16, matrix products, apply_operator(): jnp.einsum('ctj,tjk->ctk', picked, tile_values, precision=lax.Precision.H...  104 us
    gather x16, local copies, waits for them, and re-layouts, apply_operator(): picked = jnp.take(blocks, tile_cols.reshape(-1), axis=1)  27.1 us
    ppermute x64, waiting for transfers between devices, from_behind(): return lax.ppermute(block, axis, route)  22.3 us
    gather x24, local copies, waits for them, and re-layouts, apply_operator(): outgoing = jnp.take(field_in, send_list[0], axis=1)  20.6 us
    all_gather x1, blocking collectives, local(): lax.all_gather(features, 'chan', axis=0, tiled=True)  13.4 us
  transfers between devices with their start and end apart: 66, of which 18 were waited for; matrix products, arithmetic and copies ran while one was open for 26% of the time, Pallas kernels for 0%

profile of v1, /device:TPU:2, one launch (start us, length us, event | category | flops | bytes accessed | tf_op | source)
XLA Modules:
  0.0 602.3 jit_solution(6355846648055474403)
XLA Ops:
  9.0 5.7 all-to-all-start
  18.6 6.4 %collective-permute-start.33 = (f32[64,128]{0,1:T(8,128)S(1)}, f32[64,128]{0,1:T(8,128)S(1)}, u32[]{:S(2)}, u32[]{:S(2)}) collective-permute-start(f32[64,128]{0,1:T(8,128)S(1)} %get-tuple-element.34), channel_id=1, source_target_pairs={{4,0},{8,4},{12,8},{16,12},{20,16},{24,20},{28,24},{32,28},{36,32}... | collective-permute-start | bytes 98312 | tf_op jit(solution)/shard_map/ppermute | solution.py:12
  30.4 13.4 %all_gather.3 = bf16[256,1024]{1,0:T(8,128)(2,1)S(1)} all-gather(bf16[64,1024]{1,0:T(8,128)(2,1)S(1)} %copy-done.13), channel_id=1, replica_groups=mesh['dom'=64,'chan'=4] {'chan'}, dimensions={0}, use_global_device_ids=true | all-gather | bytes 655360 | tf_op jit(solution)/shard_map/all_gather | solution.py:58
  45.8 6.4 %bitcast_reduce_fusion.7 = f32[64,8,128]{2,0,1:T(8,128)} fusion(f32[64,128,128]{2,1,0:T(8,128)} %param.13, f32[64,64,128]{2,1,0:T(8,128)S(1)} %gather_fusion.17, pred[64]{0:T(512)(128)(4,1)S(1)} %compare_and_fusion), kind=kOutput, calls=%fused_computation.39 | convolution fusion | flops 806289408 | bytes 6553664 | tf_op jit(solution)/shard_map/ctj,tjk->ctk/dot_general | solution.py:32
  71.0 6.7 %bitcast_reduce_fusion.6 = f32[64,8,128]{2,0,1:T(8,128)S(1)} fusion(f32[64,128,128]{2,1,0:T(8,128)} %param.13, f32[64,64,128]{2,1,0:T(8,128)} %gather_fusion.19, pred[64]{0:T(512)(128)(4,1)S(1)} %compare_and_fusion), kind=kOutput, calls=%fused_computation.38 | convolution fusion | flops 806289408 | bytes 6553664 | tf_op jit(solution)/shard_map/ctj,tjk->ctk/dot_general | solution.py:32
  97.3 6.7 %bitcast_reduce_fusion.5 = f32[64,8,128]{2,0,1:T(8,128)S(1)} fusion(f32[64,128,128]{2,1,0:T(8,128)} %param.13, f32[64,64,128]{2,1,0:T(8,128)} %gather_fusion.21, pred[64]{0:T(512)(128)(4,1)S(1)} %compare_and_fusion), kind=kOutput, calls=%fused_computation.37 | convolution fusion | flops 806289408 | bytes 6553664 | tf_op jit(solution)/shard_map/ctj,tjk->ctk/dot_general | solution.py:32
  113.8 5.6 collective-permute-start.47
  123.7 6.7 %bitcast_reduce_fusion.4 = f32[64,8,128]{2,0,1:T(8,128)S(1)} fusion(f32[64,128,128]{2,1,0:T(8,128)} %param.13, f32[64,64,128]{2,1,0:T(8,128)} %gather_fusion.23, pred[64]{0:T(512)(128)(4,1)S(1)} %compare_and_fusion), kind=kOutput, calls=%fused_computation.36 | convolution fusion | flops 806289408 | bytes 6553664 | tf_op jit(solution)/shard_map/ctj,tjk->ctk/dot_general | solution.py:32
  139.1 5.8 collective-permute-start.51
  151.4 6.7 %bitcast_reduce_fusion.3 = f32[64,8,128]{2,0,1:T(8,128)S(1)} fusion(f32[64,128,128]{2,1,0:T(8,128)} %param.13, f32[64,64,128]{2,1,0:T(8,128)} %gather_fusion.25, pred[64]{0:T(512)(128)(4,1)S(1)} %compare_and_fusion), kind=kOutput, calls=%fused_computation.35 | convolution fusion | flops 806289408 | bytes 6553664 | tf_op jit(solution)/shard_map/ctj,tjk->ctk/dot_general | solution.py:32
  179.0 6.7 %bitcast_reduce_fusion.2 = f32[64,8,128]{2,0,1:T(8,128)S(1)} fusion(f32[64,128,128]{2,1,0:T(8,128)} %param.13, f32[64,64,128]{2,1,0:T(8,128)} %gather_fusion.27, pred[64]{0:T(512)(128)(4,1)S(1)} %compare_and_fusion), kind=kOutput, calls=%fused_computation.34 | convolution fusion | flops 806289408 | bytes 6553664 | tf_op jit(solution)/shard_map/ctj,tjk->ctk/dot_general | solution.py:32
  204.3 6.7 %bitcast_reduce_fusion.1 = f32[64,8,128]{2,0,1:T(8,128)S(1)} fusion(f32[64,128,128]{2,1,0:T(8,128)} %param.13, f32[64,64,128]{2,1,0:T(8,128)} %gather_fusion.29, pred[64]{0:T(512)(128)(4,1)S(1)} %compare_and_fusion), kind=kOutput, calls=%fused_computation.33 | convolution fusion | flops 806289408 | bytes 6553664 | tf_op jit(solution)/shard_map/ctj,tjk->ctk/dot_general | solution.py:32
  236.7 5.6 collective-permute-start.3
  246.0 6.7 %bitcast_reduce_fusion.15 = f32[64,8,128]{2,0,1:T(8,128)S(1)} fusion(f32[64,128,128]{2,1,0:T(8,128)} %param.13, f32[64,64,128]{2,1,0:T(8,128)} %gather_fusion.1, pred[64]{0:T(512)(128)(4,1)S(1)} %compare_and_fusion), kind=kOutput, calls=%fused_computation.47 | convolution fusion | flops 806289408 | bytes 6553664 | tf_op jit(solution)/shard_map/ctj,tjk->ctk/dot_general | solution.py:32
  270.1 6.7 %bitcast_reduce_fusion.14 = f32[64,8,128]{2,0,1:T(8,128)S(1)} fusion(f32[64,128,128]{2,1,0:T(8,128)} %param.13, f32[64,64,128]{2,1,0:T(8,128)} %gather_fusion.3, pred[64]{0:T(512)(128)(4,1)S(1)} %compare_and_fusion), kind=kOutput, calls=%fused_computation.46 | convolution fusion | flops 806289408 | bytes 6553664 | tf_op jit(solution)/shard_map/ctj,tjk->ctk/dot_general | solution.py:32
  298.3 6.7 %bitcast_reduce_fusion.13 = f32[64,8,128]{2,0,1:T(8,128)S(1)} fusion(f32[64,128,128]{2,1,0:T(8,128)} %param.13, f32[64,64,128]{2,1,0:T(8,128)} %gather_fusion.5, pred[64]{0:T(512)(128)(4,1)S(1)} %compare_and_fusion), kind=kOutput, calls=%fused_computation.45 | convolution fusion | flops 806289408 | bytes 6553664 | tf_op jit(solution)/shard_map/ctj,tjk->ctk/dot_general | solution.py:32
  307.5 6.7 %bitcast_reduce_fusion = f32[64,8,128]{2,0,1:T(8,128)S(1)} fusion(f32[64,128,128]{2,1,0:T(8,128)} %param.13, f32[64,64,128]{2,1,0:T(8,128)} %gather_fusion.31, pred[64]{0:T(512)(128)(4,1)S(1)} %compare_and_fusion), kind=kOutput, calls=%fused_computation.32 | convolution fusion | flops 806289408 | bytes 6553664 | tf_op jit(solution)/shard_map/ctj,tjk->ctk/dot_general | solution.py:32
  319.3 5.7 collective-permute-start.15
  328.7 6.7 %bitcast_reduce_fusion.12 = f32[64,8,128]{2,0,1:T(8,128)S(1)} fusion(f32[64,128,128]{2,1,0:T(8,128)} %param.13, f32[64,64,128]{2,1,0:T(8,128)} %gather_fusion.7, pred[64]{0:T(512)(128)(4,1)S(1)} %compare_and_fusion), kind=kOutput, calls=%fused_computation.44 | convolution fusion | flops 806289408 | bytes 6553664 | tf_op jit(solution)/shard_map/ctj,tjk->ctk/dot_general | solution.py:32
  355.5 6.7 %bitcast_reduce_fusion.11 = f32[64,8,128]{2,0,1:T(8,128)S(1)} fusion(f32[64,128,128]{2,1,0:T(8,128)} %param.13, f32[64,64,128]{2,1,0:T(8,128)} %gather_fusion.9, pred[64]{0:T(512)(128)(4,1)S(1)} %compare_and_fusion), kind=kOutput, calls=%fused_computation.43 | convolution fusion | flops 806289408 | bytes 6553664 | tf_op jit(solution)/shard_map/ctj,tjk->ctk/dot_general | solution.py:32
  380.9 5.7 bitcast_reduce_fusion.10
  403.7 5.7 bitcast_reduce_fusion.9
  411.9 162.8 %all-reduce.2.cloned.1.call-done = f32[9,256,64]{1,2,0:T(8,128)} async-done(((f32[9,256,64]{1,2,0:T(8,128)}), f32[9,256,64]{1,2,0:T(8,128)}) %all-reduce.2.cloned.1.call-update) | async-done | bytes 589840 | tf_op jit(solution)/shard_map/psum | solution.py:87
  587.9 5.7 bitcast_reduce_fusion.8
  (368 shorter events, 271.7 us)
Async XLA Ops:
  9.0 217.8 %all-to-all-start = ((bf16[4,64,1024]{2,1,0:T(8,128)(2,1)}), bf16[4,64,1024]{2,1,0:T(8,128)(2,1)S(1)}, u32[]{:S(2)}, u32[]{:S(2)}) async-start(bf16[4,64,1024]{2,1,0:T(8,128)(2,1)} %tile.2), calls=%async_computation | async-start | bytes 1048576 | tf_op jit(solution)/shard_map/all_to_all | solution.py:47
  14.7 560.0 %all-reduce.2.cloned.1.call-start = ((), (), s32[]{:S(2)}) async-start(), calls=%async_computation.1 | async-start | bytes 1179648 | tf_op jit(solution)/shard_map/psum | solution.py:87
  18.5 26.3 %collective-permute-start.32 = (f32[64,128]{0,1:T(8,128)S(1)}, f32[64,128]{0,1:T(8,128)S(1)}, u32[]{:S(2)}, u32[]{:S(2)}) collective-permute-start(f32[64,128]{0,1:T(8,128)S(1)} %get-tuple-element.35), channel_id=1, source_target_pairs={{252,0},{0,4},{4,8},{8,12},{12,16},{16,20},{20,24},{24,28},{28,32}... | collective-permute-start | bytes 98312 | tf_op jit(solution)/shard_map/ppermute | solution.py:12
  18.6 26.2 %collective-permute-start.33 = (f32[64,128]{0,1:T(8,128)S(1)}, f32[64,128]{0,1:T(8,128)S(1)}, u32[]{:S(2)}, u32[]{:S(2)}) collective-permute-start(f32[64,128]{0,1:T(8,128)S(1)} %get-tuple-element.34), channel_id=1, source_target_pairs={{4,0},{8,4},{12,8},{16,12},{20,16},{24,20},{28,24},{32,28},{36,32}... | collective-permute-start | bytes 98312 | tf_op jit(solution)/shard_map/ppermute | solution.py:12
  25.0 19.8 %collective-permute-start.34 = (f32[64,128]{0,1:T(8,128)S(1)}, f32[64,128]{0,1:T(8,128)S(1)}, u32[]{:S(2)}, u32[]{:S(2)}) collective-permute-start(f32[64,128]{0,1:T(8,128)S(1)} %get-tuple-element.33), channel_id=1, source_target_pairs={{248,0},{252,4},{0,8},{4,12},{8,16},{12,20},{16,24},{20,28},{24,32... | collective-permute-start | bytes 98312 | tf_op jit(solution)/shard_map/ppermute | solution.py:12
  25.0 19.8 %collective-permute-start.35 = (f32[64,128]{0,1:T(8,128)S(1)}, f32[64,128]{0,1:T(8,128)S(1)}, u32[]{:S(2)}, u32[]{:S(2)}) collective-permute-start(f32[64,128]{0,1:T(8,128)S(1)} %get-tuple-element.32), channel_id=1, source_target_pairs={{8,0},{12,4},{16,8},{20,12},{24,16},{28,20},{32,24},{36,28},{40,32... | collective-permute-start | bytes 98312 | tf_op jit(solution)/shard_map/ppermute | solution.py:12
  81.1 11.9 %collective-permute-start.40 = (f32[64,128]{0,1:T(8,128)S(1)}, f32[64,128]{0,1:T(8,128)S(1)}, u32[]{:S(2)}, u32[]{:S(2)}) collective-permute-start(f32[64,128]{0,1:T(8,128)S(1)} %get-tuple-element.27), channel_id=1, source_target_pairs={{252,0},{0,4},{4,8},{8,12},{12,16},{16,20},{20,24},{24,28},{28,32}... | collective-permute-start | bytes 98312 | tf_op jit(solution)/shard_map/ppermute | solution.py:12
  107.5 11.9 %collective-permute-start.44 = (f32[64,128]{0,1:T(8,128)S(1)}, f32[64,128]{0,1:T(8,128)S(1)}, u32[]{:S(2)}, u32[]{:S(2)}) collective-permute-start(f32[64,128]{0,1:T(8,128)S(1)} %get-tuple-element.23), channel_id=1, source_target_pairs={{252,0},{0,4},{4,8},{8,12},{12,16},{16,20},{20,24},{24,28},{28,32}... | collective-permute-start | bytes 98312 | tf_op jit(solution)/shard_map/ppermute | solution.py:12
  132.7 12.2 %collective-permute-start.48 = (f32[64,128]{0,1:T(8,128)S(1)}, f32[64,128]{0,1:T(8,128)S(1)}, u32[]{:S(2)}, u32[]{:S(2)}) collective-permute-start(f32[64,128]{0,1:T(8,128)S(1)} %get-tuple-element.19), channel_id=1, source_target_pairs={{252,0},{0,4},{4,8},{8,12},{12,16},{16,20},{20,24},{24,28},{28,32}... | collective-permute-start | bytes 98312 | tf_op jit(solution)/shard_map/ppermute | solution.py:12
  134.1 11.5 %collective-permute-start.49 = (f32[64,128]{0,1:T(8,128)S(1)}, f32[64,128]{0,1:T(8,128)S(1)}, u32[]{:S(2)}, u32[]{:S(2)}) collective-permute-start(f32[64,128]{0,1:T(8,128)S(1)} %get-tuple-element.18), channel_id=1, source_target_pairs={{4,0},{8,4},{12,8},{16,12},{20,16},{24,20},{28,24},{32,28},{36,32}... | collective-permute-start | bytes 98312 | tf_op jit(solution)/shard_map/ppermute | solution.py:12
  160.4 11.9 %collective-permute-start.52 = (f32[64,128]{0,1:T(8,128)S(1)}, f32[64,128]{0,1:T(8,128)S(1)}, u32[]{:S(2)}, u32[]{:S(2)}) collective-permute-start(f32[64,128]{0,1:T(8,128)S(1)} %get-tuple-element.15), channel_id=1, source_target_pairs={{252,0},{0,4},{4,8},{8,12},{12,16},{16,20},{20,24},{24,28},{28,32}... | collective-permute-start | bytes 98312 | tf_op jit(solution)/shard_map/ppermute | solution.py:12
  161.7 11.2 %collective-permute-start.53 = (f32[64,128]{0,1:T(8,128)S(1)}, f32[64,128]{0,1:T(8,128)S(1)}, u32[]{:S(2)}, u32[]{:S(2)}) collective-permute-start(f32[64,128]{0,1:T(8,128)S(1)} %get-tuple-element.14), channel_id=1, source_target_pairs={{4,0},{8,4},{12,8},{16,12},{20,16},{24,20},{28,24},{32,28},{36,32}... | collective-permute-start | bytes 98312 | tf_op jit(solution)/shard_map/ppermute | solution.py:12
  188.1 11.9 %collective-permute-start.56 = (f32[64,128]{0,1:T(8,128)S(1)}, f32[64,128]{0,1:T(8,128)S(1)}, u32[]{:S(2)}, u32[]{:S(2)}) collective-permute-start(f32[64,128]{0,1:T(8,128)S(1)} %get-tuple-element.11), channel_id=1, source_target_pairs={{252,0},{0,4},{4,8},{8,12},{12,16},{16,20},{20,24},{24,28},{28,32}... | collective-permute-start | bytes 98312 | tf_op jit(solution)/shard_map/ppermute | solution.py:12
  215.1 11.6 %collective-permute-start.60 = (f32[64,128]{0,1:T(8,128)S(1)}, f32[64,128]{0,1:T(8,128)S(1)}, u32[]{:S(2)}, u32[]{:S(2)}) collective-permute-start(f32[64,128]{0,1:T(8,128)S(1)} %get-tuple-element.7), channel_id=1, source_target_pairs={{252,0},{0,4},{4,8},{8,12},{12,16},{16,20},{20,24},{24,28},{28,32}... | collective-permute-start | bytes 98312 | tf_op jit(solution)/shard_map/ppermute | solution.py:12
  216.3 13.8 %collective-permute-start.61 = (f32[64,128]{0,1:T(8,128)}, f32[64,128]{0,1:T(8,128)}, u32[]{:S(2)}, u32[]{:S(2)}) collective-permute-start(f32[64,128]{0,1:T(8,128)} %get-tuple-element.6), channel_id=1, source_target_pairs={{4,0},{8,4},{12,8},{16,12},{20,16},{24,20},{28,24},{32,28},{36,32}... | collective-permute-start | bytes 98312 | tf_op jit(solution)/shard_map/ppermute | solution.py:12
  221.3 33.8 %collective-permute-start.62 = (f32[64,128]{0,1:T(8,128)}, f32[64,128]{0,1:T(8,128)S(1)}, u32[]{:S(2)}, u32[]{:S(2)}) collective-permute-start(f32[64,128]{0,1:T(8,128)} %get-tuple-element.5), channel_id=1, source_target_pairs={{248,0},{252,4},{0,8},{4,12},{8,16},{12,20},{16,24},{20,28},{24,32... | collective-permute-start | bytes 98312 | tf_op jit(solution)/shard_map/ppermute | solution.py:12
  221.3 60.2 %collective-permute-start.63 = (f32[64,128]{0,1:T(8,128)}, f32[64,128]{0,1:T(8,128)S(1)}, u32[]{:S(2)}, u32[]{:S(2)}) collective-permute-start(f32[64,128]{0,1:T(8,128)} %get-tuple-element.4), channel_id=1, source_target_pairs={{8,0},{12,4},{16,8},{20,12},{24,16},{28,20},{32,24},{36,28},{40,32... | collective-permute-start | bytes 98312 | tf_op jit(solution)/shard_map/ppermute | solution.py:12
  255.1 11.3 %collective-permute-start.4 = (f32[64,128]{1,0:T(8,128)S(1)}, f32[64,128]{1,0:T(8,128)S(1)}, u32[]{:S(2)}, u32[]{:S(2)}) collective-permute-start(f32[64,128]{1,0:T(8,128)S(1)} %get-tuple-element.63), channel_id=1, source_target_pairs={{252,0},{0,4},{4,8},{8,12},{12,16},{16,20},{20,24},{24,28},{28,32}... | collective-permute-start | bytes 98312 | tf_op jit(solution)/shard_map/ppermute | solution.py:12
  281.5 13.0 %collective-permute-start.8 = (f32[64,128]{1,0:T(8,128)S(1)}, f32[64,128]{1,0:T(8,128)S(1)}, u32[]{:S(2)}, u32[]{:S(2)}) collective-permute-start(f32[64,128]{1,0:T(8,128)S(1)} %get-tuple-element.59), channel_id=1, source_target_pairs={{252,0},{0,4},{4,8},{8,12},{12,16},{16,20},{20,24},{24,28},{28,32}... | collective-permute-start | bytes 98312 | tf_op jit(solution)/shard_map/ppermute | solution.py:12
  307.4 17.6 %collective-permute-start.12 = (f32[64,128]{1,0:T(8,128)S(1)}, f32[64,128]{1,0:T(8,128)S(1)}, u32[]{:S(2)}, u32[]{:S(2)}) collective-permute-start(f32[64,128]{1,0:T(8,128)S(1)} %get-tuple-element.55), channel_id=1, source_target_pairs={{252,0},{0,4},{4,8},{8,12},{12,16},{16,20},{20,24},{24,28},{28,32}... | collective-permute-start | bytes 98312 | tf_op jit(solution)/shard_map/ppermute | solution.py:12
  338.8 11.2 %collective-permute-start.17 = (f32[64,128]{1,0:T(8,128)S(1)}, f32[64,128]{1,0:T(8,128)S(1)}, u32[]{:S(2)}, u32[]{:S(2)}) collective-permute-start(f32[64,128]{1,0:T(8,128)S(1)} %get-tuple-element.50), channel_id=1, source_target_pairs={{4,0},{8,4},{12,8},{16,12},{20,16},{24,20},{28,24},{32,28},{36,32}... | collective-permute-start | bytes 98312 | tf_op jit(solution)/shard_map/ppermute | solution.py:12
  366.8 11.4 %collective-permute-start.20 = (f32[64,128]{1,0:T(8,128)S(1)}, f32[64,128]{1,0:T(8,128)S(1)}, u32[]{:S(2)}, u32[]{:S(2)}) collective-permute-start(f32[64,128]{1,0:T(8,128)S(1)} %get-tuple-element.47), channel_id=1, source_target_pairs={{252,0},{0,4},{4,8},{8,12},{12,16},{16,20},{20,24},{24,28},{28,32}... | collective-permute-start | bytes 98312 | tf_op jit(solution)/shard_map/ppermute | solution.py:12
  389.0 12.0 %collective-permute-start.24 = (f32[64,128]{1,0:T(8,128)S(1)}, f32[64,128]{1,0:T(8,128)S(1)}, u32[]{:S(2)}, u32[]{:S(2)}) collective-permute-start(f32[64,128]{1,0:T(8,128)S(1)} %get-tuple-element.43), channel_id=1, source_target_pairs={{252,0},{0,4},{4,8},{8,12},{12,16},{16,20},{20,24},{24,28},{28,32}... | collective-permute-start | bytes 98312 | tf_op jit(solution)/shard_map/ppermute | solution.py:12
  411.8 173.4 %collective-permute-start.28 = (f32[64,128]{1,0:T(8,128)S(1)}, f32[64,128]{1,0:T(8,128)S(1)}, u32[]{:S(2)}, u32[]{:S(2)}) collective-permute-start(f32[64,128]{1,0:T(8,128)S(1)} %get-tuple-element.39), channel_id=1, source_target_pairs={{252,0},{0,4},{4,8},{8,12},{12,16},{16,20},{20,24},{24,28},{28,32}... | collective-permute-start | bytes 98312 | tf_op jit(solution)/shard_map/ppermute | solution.py:12
  (57 other events, 501.4 us)
Sparse Core Ops, SparseCore 0:
  390.5 184.1 all-reduce.1
